TPU v7x, 32 devices: a whole 2x2x4 slice. The times are simulated.
32 devices in a mesh: group: 2 (over y), context: 4 (over z), head: 4 (over x, core).
Axes of the slice: x: 2, y: 2, z: 4, core: 2. Of those that a mesh axis runs over, the one named last changes fastest.
Arguments:
- dn_query: bfloat16 [1024, 2048], P(('group', 'context'), 'head'), parts along dimension 0, may hold values from -6 to 6
- dn_key: bfloat16 [1024, 2048], P(('group', 'context'), 'head'), parts along dimension 0, may hold values from -6 to 6
- dn_value: bfloat16 [1024, 4096], P(('group', 'context'), 'head'), parts along dimension 0, may hold values from -6 to 6
- dn_gate: bfloat16 [1024, 4096], P(('group', 'context'), 'head'), parts along dimension 0, may hold values from -6 to 6
- dn_beta_logit: float32 [1024, 32], P(('group', 'context'), 'head'), parts along dimension 0, may hold values from -6 to 6
- dn_decay: float32 [1024, 32], P(('group', 'context'), 'head'), parts along dimension 0, may hold values from -1 to 0
- dn_norm_gain: float32 [128], replicated, may hold values from 0.1 to 1.9
- prefix_state: bfloat16 [4, 32, 128, 128], P('group', 'head', 'context'), parts along dimension 0, may hold values from -6 to 6
- at_query: bfloat16 [1024, 4096], P(('group', 'context'), 'head'), parts along dimension 0, may hold values from -6 to 6
- at_gate: bfloat16 [1024, 4096], P(('group', 'context'), 'head'), parts along dimension 0, may hold values from -6 to 6
- at_key: bfloat16 [1024, 512], P(('group', 'context')), parts along dimension 0, may hold values from -6 to 6
- at_value: bfloat16 [1024, 512], P(('group', 'context')), parts along dimension 0, may hold values from -6 to 6
- prefix_key: bfloat16 [16, 64, 512], P(('group', 'context')), parts along dimension 0, may hold values from -6 to 6
- prefix_value: bfloat16 [16, 64, 512], P(('group', 'context')), parts along dimension 0, may hold values from -6 to 6
- req_len: int32 [8], P('group'), parts along dimension 0, may hold values from 1 to 256, 512 in all
- req_prefix: int32 [8], P('group'), parts along dimension 0, may hold values from 0 to 1, as said below
- req_offset: int32 [8], P('group'), parts along dimension 0, may hold values from 64 to 256, as said below
- block_table: int32 [16], P('group'), parts along dimension 0, may hold values from 0 to 7, each once
Outputs:
- dn_out: bfloat16 [1024, 4096], P(('group', 'context'), 'head'), parts along dimension 0
- at_out: bfloat16 [1024, 4096], P(('group', 'context'), 'head'), parts along dimension 0
There are 2 independent parts, one for each index of `group`. A program takes and returns all parts, laid end to end along the dimension named above; an argument that names none is the same for every part. Nothing has to cross between parts.
Inputs may be any that keep to these rules, and one draw needn't show every extreme that they name: `req_len`: requests lie one after another in row order; the longest has exactly 256 new tokens. `req_prefix`: every prefix is extended by one or more requests. `req_offset`: equal for the requests of one prefix: the number of its cached positions; one prefix holds 256, another from a quarter to a half of 256. `block_table`: entry p * 4 + j is the slot of block j of prefix p; every slot once.
All inputs are finite; a program needn't handle non-finite values.
Results may differ from a plain program's by a relative error of at most 0.011.
Values may be sent and summed in bfloat16 or wider, within the bound.
A program may use at most 128 MiB of HBM per device.

v0:
```python
import math
import jax
import jax.numpy as jnp
from jax import lax
from jax.sharding import PartitionSpec as P

VH = 32
KH = 16
DK = 128
DV = 128
HQ = 16
KVH = 2
HD = 256
ROT = 64
ROPE_THETA = 10000000.0
YARN_FACTOR = 4.0
YARN_ANCHOR = 262144.0
NEG_LARGE = -1e30
HIGH = lax.Precision.HIGHEST


def carried_in(x, axis, join, neutral):
    place = lax.axis_index(axis)
    gathered = jax.tree.map(
        lambda a, kind: lax.all_gather(a.astype(kind), axis),
        x,
        (jnp.bfloat16, jnp.bfloat16, jnp.bfloat16),
    )
    state = jax.tree.map(lambda a, e: jnp.zeros_like(a) + jnp.asarray(e, a.dtype), x, neutral)

    def one(turn, state):
        return join(
            state,
            jax.tree.map(
                lambda a, own: lax.dynamic_index_in_dim(a, turn, 0, False).astype(own.dtype),
                gathered,
                x,
            ),
        )

    return lax.fori_loop(0, place, one, state)


def yarn_tables(positions, rotary):
    half = rotary // 2
    log_theta = math.log(ROPE_THETA)
    lower = max(
        math.floor(rotary * math.log(YARN_ANCHOR / (64.0 * math.pi)) / (2.0 * log_theta)), 0
    )
    upper = min(
        math.ceil(rotary * math.log(YARN_ANCHOR / (2.0 * math.pi)) / (2.0 * log_theta)), rotary - 1
    )
    spread = float(upper - lower)
    index = jnp.arange(half, dtype=jnp.float32)
    plain_frequency = jnp.exp(index * (-2.0 * log_theta / rotary))
    keep = 1.0 - jnp.clip((index - lower) / spread, 0.0, 1.0)
    frequency = plain_frequency * keep + plain_frequency / YARN_FACTOR * (1.0 - keep)
    angles = positions.astype(jnp.float32)[:, None] * frequency[None, :]
    attention_factor = 0.1 * math.log(YARN_FACTOR) + 1.0
    return (jnp.cos(angles) * attention_factor, jnp.sin(angles) * attention_factor)


def rotate(values, cosines, sines, rotary):
    half = rotary // 2
    first = values[..., :half]
    second = values[..., half:rotary]
    cosines = cosines[:, None, :]
    sines = sines[:, None, :]
    return jnp.concatenate(
        [first * cosines - second * sines, second * cosines + first * sines, values[..., rotary:]],
        axis=-1,
    )


def unit_rows(values):
    return values * lax.rsqrt(jnp.sum(values * values, axis=-1, keepdims=True) + 1e-06)


def row_layout(rows, req_len, req_prefix, req_offset):
    starts = jnp.cumsum(req_len) - req_len
    leading_found = (starts[None, :] <= rows[:, None]).astype(jnp.int32)
    segment = jnp.sum(leading_found, axis=1) - 1
    choose = (segment[:, None] == jnp.arange(req_len.shape[0], dtype=jnp.int32)[None, :]).astype(
        jnp.int32
    )
    first = jnp.sum(choose * starts[None, :], axis=1)
    prefix = jnp.sum(choose * req_prefix[None, :], axis=1)
    offset = jnp.sum(choose * req_offset[None, :], axis=1)
    return (segment, first, prefix, offset, offset + rows - first)


def absorb(state, queries, search_handles, values, visible):
    peak, total, summed = state
    scores = jnp.einsum(
        "thd,nd->thn", queries, search_handles, preferred_element_type=jnp.float32
    ) * search_handles.shape[-1] ** (-0.5)
    seen = visible[:, None, :]
    scores = jnp.where(seen, scores, NEG_LARGE)
    new_peak = jnp.maximum(peak, jnp.max(scores, axis=-1))
    weights = jnp.where(seen, jnp.exp(scores - new_peak[..., None]), 0.0)
    shrink = jnp.exp(peak - new_peak)
    total = total * shrink + jnp.sum(weights, axis=-1)
    summed = summed * shrink[..., None] + jnp.einsum(
        "thn,nd->thd", weights.astype(jnp.bfloat16), values, preferred_element_type=jnp.float32
    )
    return (new_peak, total, summed)


def compose(earlier, later):
    map_early, add_early, flag_early = earlier
    map_late, add_late, flag_late = later
    fresh = flag_late > 0.5
    joined_map = jnp.where(
        fresh, map_late, jnp.einsum("hij,hjk->hik", map_early, map_late, precision=HIGH)
    )
    joined_add = jnp.where(
        fresh, add_late, jnp.einsum("hvj,hjk->hvk", add_early, map_late, precision=HIGH) + add_late
    )
    return (joined_map, joined_add, jnp.maximum(flag_early, flag_late))


def shards(
    dn_query,
    dn_key,
    dn_value,
    dn_gate,
    dn_beta_logit,
    dn_decay,
    dn_norm_gain,
    prefix_state,
    at_query,
    at_gate,
    at_key,
    at_value,
    prefix_key,
    prefix_value,
    req_len,
    req_prefix,
    req_offset,
    block_table,
):
    tokens_here = dn_query.shape[0]
    key_heads = dn_query.shape[1] // DK
    value_heads = dn_value.shape[1] // DV
    query_heads = at_query.shape[1] // HD
    device = lax.axis_index("context")
    row_start = device * tokens_here
    rows = row_start + jnp.arange(tokens_here, dtype=jnp.int32)
    segment, first, prefix, offset, position = row_layout(rows, req_len, req_prefix, req_offset)
    query = jnp.repeat(
        unit_rows(dn_query.reshape(tokens_here, key_heads, DK).astype(jnp.float32)) * DK ** (-0.5),
        VH // KH,
        axis=1,
    )
    key = jnp.repeat(
        unit_rows(dn_key.reshape(tokens_here, key_heads, DK).astype(jnp.float32)), VH // KH, axis=1
    )
    query_heads_first = jnp.transpose(query, (1, 0, 2))
    key_heads_first = jnp.transpose(key, (1, 0, 2))
    value_heads_first = jnp.transpose(
        dn_value.reshape(tokens_here, value_heads, DV).astype(jnp.float32), (1, 0, 2)
    )
    beta = jax.nn.sigmoid(dn_beta_logit).T
    same = segment[:, None] == segment[None, :]
    causal = same & (rows[:, None] >= rows[None, :])
    strict = same & (rows[:, None] > rows[None, :])
    running = jnp.dot(causal.astype(jnp.float32), dn_decay, precision=HIGH).T
    gaps = running[:, :, None] - running[:, None, :]
    decay_mat = jnp.where(causal[None], jnp.exp(jnp.where(causal[None], gaps, 0.0)), 0.0)
    key_gram = jnp.einsum("hid,hjd->hij", key_heads_first, key_heads_first, precision=HIGH)
    query_key = jnp.einsum("hid,hjd->hij", query_heads_first, key_heads_first, precision=HIGH)
    lower_mat = jnp.where(strict[None], beta[:, :, None] * key_gram * decay_mat, 0.0)
    system = jnp.eye(tokens_here, dtype=jnp.float32)[None] + lower_mat
    start_decay = jnp.exp(running)
    solve_values = beta[:, :, None] * value_heads_first
    solve_keys = (beta * start_decay)[:, :, None] * key_heads_first
    solved = jax.scipy.linalg.solve_triangular(
        system, jnp.concatenate([solve_values, solve_keys], axis=2), lower=True, unit_diagonal=True
    )
    update = solved[:, :, :DV]
    wy_keys = solved[:, :, DV:]
    mixing = decay_mat * query_key
    local_out = jnp.einsum("hij,hjv->hiv", mixing, update, precision=HIGH)
    reach = start_decay[:, :, None] * query_heads_first - jnp.einsum(
        "hij,hjk->hik", mixing, wy_keys, precision=HIGH
    )
    tail = segment == segment[tokens_here - 1]
    end_gaps = running[:, tokens_here - 1 : tokens_here] - running
    end_weight = jnp.where(tail[None, :], jnp.exp(jnp.where(tail[None, :], end_gaps, 0.0)), 0.0)
    end_decay = start_decay[:, tokens_here - 1]
    identity_mat = jnp.eye(DK, dtype=jnp.float32)
    carry_map = end_decay[:, None, None] * identity_mat[None] - jnp.einsum(
        "hjk,hj,hjl->hkl", wy_keys, end_weight, key_heads_first, precision=HIGH
    )
    carry_add = jnp.einsum("hjv,hj,hjl->hvl", update, end_weight, key_heads_first, precision=HIGH)
    restart = (first[tokens_here - 1] >= row_start).astype(jnp.float32)
    identity = (
        jnp.broadcast_to(identity_mat, (value_heads, DK, DK)),
        jnp.zeros((value_heads, DV, DK), jnp.float32),
        jnp.zeros((), jnp.float32),
    )
    into_map, into_add, into_flag = carried_in(
        (carry_map, carry_add, restart), "context", compose, identity
    )
    carried = ((segment == segment[0]) & (first[0] < row_start))[None, :, None]
    through = jnp.einsum("hkl,hil->hik", into_map, reach, precision=HIGH)
    extra = jnp.einsum("hvk,hik->hiv", into_add, reach, precision=HIGH)
    weight_vec = jnp.where(carried, through, reach).astype(jnp.bfloat16)
    core = local_out + jnp.where(carried, extra, 0.0)
    owner_ids = jnp.arange(prefix_state.shape[0], dtype=jnp.int32)
    select = (prefix[None, :] == owner_ids[:, None]).astype(jnp.bfloat16)
    masked = select[:, None, :, None] * weight_vec[None]
    state_part = jnp.einsum(
        "phik,phvk->hiv",
        masked,
        lax.all_gather(prefix_state, "context", axis=2, tiled=True),
        preferred_element_type=jnp.float32,
    )
    core = core + state_part
    core_rows = jnp.transpose(core, (1, 0, 2))
    normed = core_rows * lax.rsqrt(jnp.mean(core_rows * core_rows, axis=-1, keepdims=True) + 1e-06)
    gate_rows = dn_gate.reshape(tokens_here, value_heads, DV).astype(jnp.float32)
    dn_out = (
        (normed * dn_norm_gain * jax.nn.silu(gate_rows))
        .reshape(tokens_here, value_heads * DV)
        .astype(jnp.bfloat16)
    )
    group = HQ // KVH
    kv_head = lax.axis_index("head") * query_heads // group
    cosines, sines = yarn_tables(position, ROT)
    query_rot = rotate(
        at_query.reshape(tokens_here, query_heads, HD).astype(jnp.float32), cosines, sines, ROT
    ).astype(jnp.bfloat16)
    new_key = lax.dynamic_slice_in_dim(at_key, kv_head * HD, HD, 1).reshape(tokens_here, 1, HD)
    new_key = (
        rotate(new_key.astype(jnp.float32), cosines, sines, ROT)
        .reshape(tokens_here, HD)
        .astype(jnp.bfloat16)
    )
    new_value = lax.dynamic_slice_in_dim(at_value, kv_head * HD, HD, 1)
    cached_key = lax.dynamic_slice_in_dim(prefix_key, kv_head * HD, HD, 2)
    cached_value = lax.dynamic_slice_in_dim(prefix_value, kv_head * HD, HD, 2)
    table_index = jnp.arange(block_table.shape[0], dtype=jnp.int32)
    blocks_per_prefix = block_table.shape[0] // prefix_state.shape[0]
    state = (
        jnp.full((tokens_here, query_heads), NEG_LARGE, jnp.float32),
        jnp.zeros((tokens_here, query_heads), jnp.float32),
        jnp.zeros((tokens_here, query_heads, HD), jnp.float32),
    )
    search_handles = lax.all_gather(cached_key, "context", axis=0, tiled=True)
    values = lax.all_gather(cached_value, "context", axis=0, tiled=True)
    count = search_handles.shape[0]
    width = search_handles.shape[1]
    slots = jnp.arange(count, dtype=jnp.int32)
    entry = jnp.sum(
        jnp.where(block_table[None, :] == slots[:, None], table_index[None, :], 0), axis=1
    )
    owner = jnp.repeat(entry // blocks_per_prefix, width)
    where_in = (
        (entry % blocks_per_prefix)[:, None] * width + jnp.arange(width, dtype=jnp.int32)[None, :]
    ).reshape(count * width)
    visible = (owner[None, :] == prefix[:, None]) & (where_in[None, :] < offset[:, None])
    flat_keys = search_handles.reshape(count * width, search_handles.shape[2])
    flat_values = values.reshape(count * width, values.shape[2])
    state = absorb(state, query_rot, flat_keys, flat_values, visible)
    search_handles = lax.all_gather(new_key, "context", axis=0, tiled=True)
    values = lax.all_gather(new_value, "context", axis=0, tiled=True)
    key_rows = jnp.arange(search_handles.shape[0], dtype=jnp.int32)
    key_segment = row_layout(key_rows, req_len, req_prefix, req_offset)[0]
    visible = (key_segment[None, :] == segment[:, None]) & (key_rows[None, :] <= rows[:, None])
    state = absorb(state, query_rot, search_handles, values, visible)
    peak, total, summed = state
    attention = summed / total[..., None]
    gate_att = at_gate.reshape(tokens_here, query_heads, HD).astype(jnp.float32)
    at_out = (
        (attention * jax.nn.sigmoid(gate_att))
        .reshape(tokens_here, query_heads * HD)
        .astype(jnp.bfloat16)
    )
    return (dn_out, at_out)


def solution(mesh):
    placed = (
        P(("group", "context"), "head"),
        P(("group", "context"), "head"),
        P(("group", "context"), "head"),
        P(("group", "context"), "head"),
        P(("group", "context"), "head"),
        P(("group", "context"), "head"),
        P(),
        P("group", "head", "context", None),
        P(("group", "context"), "head"),
        P(("group", "context"), "head"),
        P(("group", "context"), None),
        P(("group", "context"), None),
        P(("group", "context"), None, None),
        P(("group", "context"), None, None),
        P("group"),
        P("group"),
        P("group"),
        P("group"),
    )
    return jax.shard_map(
        shards,
        mesh=mesh,
        in_specs=placed,
        out_specs=(P(("group", "context"), "head"), P(("group", "context"), "head")),
        check_vma=False,
    )
```

profile of v0, /device:TPU:26, one launch (start us, length us, event | category | flops | bytes accessed | tf_op | source)
XLA Modules:
  0.0 243.3 jit_solution(15976261732324481945)
XLA Ops:
  7.3 0.7 copy-done.35
  8.3 0.7 fusion.73
  9.1 0.7 fusion.74
  11.4 0.6 copy-done.25
  12.8 2.1 fusion.15
  14.9 79.4 %custom-call.4 = f32[8,1,128,128]{2,3,1,0:T(8,128)S(1)} custom-call(f32[8,1,128,128]{3,2,1,0:T(8,128)} %fusion.15), custom_call_target="InvertDiagBlocksLowerTriangular" | custom-call | tf_op jit(solution)/shard_map/jit(_solve_triangular)/vmap()/triangular_solve | solution.py:177
  94.3 1.8 compare_and_fusion.3
  96.7 1.0 fusion.22
  97.8 1.7 convolution_convert_fusion
  99.8 1.7 fusion.20
  101.6 0.8 copy-done.11
  102.8 0.8 slice.68
  104.2 16.7 %all-gather.2 = bf16[512,1,256]{0,2,1:T(8,128)(2,1)} all-gather(bf16[128,1,256]{0,2,1:T(8,128)(2,1)S(1)} %pad_maximum_fusion.1), channel_id=4, replica_groups=mesh['group'=2,'context'=4,'head'=4] {'context'}, dimensions={0}, use_global_device_ids=true | all-gather | bytes 327680 | tf_op jit(solution)/shard_map/all_gather | solution.py:266
  121.1 0.7 fusion.49
  121.9 16.6 %all_gather.40 = bf16[8,64,256]{2,1,0:T(8,128)(2,1)} all-gather(bf16[2,64,256]{2,1,0:T(8,128)(2,1)S(1)} %constant_dynamic-slice_fusion.3), channel_id=1, replica_groups=mesh['group'=2,'context'=4,'head'=4] {'context'}, dimensions={0}, use_global_device_ids=true | all-gather | bytes 327680 | tf_op jit(solution)/shard_map/all_gather | solution.py:250
  138.9 16.8 %all_gather.41 = bf16[8,64,256]{2,1,0:T(8,128)(2,1)} all-gather(bf16[2,64,256]{2,1,0:T(8,128)(2,1)S(1)} %constant_dynamic-slice_fusion.2), channel_id=1, replica_groups=mesh['group'=2,'context'=4,'head'=4] {'context'}, dimensions={0}, use_global_device_ids=true | all-gather | bytes 327680 | tf_op jit(solution)/shard_map/all_gather | solution.py:251
  155.7 16.5 %all_gather.43 = bf16[512,256]{1,0:T(8,128)(2,1)} all-gather(bf16[128,256]{1,0:T(8,128)(2,1)S(1)} %constant_dynamic-slice_fusion.4), channel_id=1, replica_groups=mesh['group'=2,'context'=4,'head'=4] {'context'}, dimensions={0}, use_global_device_ids=true | all-gather | bytes 327680 | tf_op jit(solution)/shard_map/all_gather | solution.py:267
  172.5 1.0 copy.164
  173.6 0.8 multiply_reduce_fusion.2
  175.5 0.6 copy-done.5
  178.2 0.7 fusion.26
  179.5 0.6 dynamic-slice
  180.1 1.2 fusion.18
  181.8 1.9 dynamic-update-slice
  183.7 2.3 fusion.19
  186.0 0.6 copy-done.39
  186.6 8.6 %all-reduce = bf16[4]{0:T(256)(128)(2,1)} all-reduce(bf16[4]{0:T(256)(128)(2,1)S(1)} %copy-done.39), channel_id=1, replica_groups=mesh['group'=2,'context'=4,'head'=4] {'context'}, use_global_device_ids=true, to_apply=%add | all-reduce | flops 4 | bytes 16
  195.3 1.1 copy.165
  196.4 0.9 copy.167
  197.5 0.9 copy-done.17
  198.4 0.9 copy-done.13
  199.7 15.1 %all_gather.39 = bf16[2,8,128,128]{3,2,0,1:T(8,128)(2,1)S(1)} all-gather(bf16[2,8,32,128]{3,2,0,1:T(8,128)(2,1)S(1)} %copy.150), channel_id=1, replica_groups=mesh['group'=2,'context'=4,'head'=4] {'context'}, dimensions={2}, use_global_device_ids=true | all-gather | bytes 655360 | tf_op jit(solution)/shard_map/all_gather | solution.py:216
  215.5 0.6 copy-done.19
  216.1 1.2 convolution_multiply_fusion.3
  217.3 1.5 fusion.43
  218.8 0.7 convolution_subtract_fusion.1
  220.2 11.2 %while.14 = (s32[]{:T(128)}, f32[8,128,128]{1,2,0:T(8,128)S(1)}, f32[8,128,128]{1,2,0:T(8,128)S(1)}, s32[]{:T(128)}, bf16[4]{0:T(256)(128)(2,1)S(1)}, /*index=5*...) while((s32[]{:T(128)}, f32[8,128,128]{1,2,0:T(8,128)S(1)}, ...), condition=%wide.region_6.7_spmd, body=%wide.region_5.6_spmd.sunk | while | flops 403308544 | bytes 7340196 | solution.py:41
  220.2 1.1 constant_dynamic-slice_fusion.7
  221.4 0.6 dynamic_slice.39
  223.9 1.1 constant_dynamic-slice_fusion.7
  225.2 0.6 dynamic_slice.39
  227.7 1.1 constant_dynamic-slice_fusion.7
  228.9 0.6 dynamic_slice.39
  232.0 0.7 fusion.21
  233.0 0.7 copy-done.1
  233.7 0.8 multiply_reduce_fusion
  234.6 0.6 copy-done.30
  235.6 0.9 copy.166
  (167 shorter events, 15.8 us)
Async XLA Ops:
  7.2 96.5 %copy-start = (bf16[128,512]{1,0:T(8,128)(2,1)S(1)}, bf16[128,512]{1,0:T(8,128)(2,1)}, u32[]{:S(2)}) copy-start(bf16[128,512]{1,0:T(8,128)(2,1)} %param.30) | copy-start | bytes 393220
  7.2 212.3 %all-gather.8.cloned.1.call-start = ((), (), s32[]{:S(2)}) async-start(), calls=%async_computation.1 | async-start | bytes 1310720 | tf_op jit(solution)/shard_map/all_gather | solution.py:25
  7.2 3.6 %copy-start.15 = (bf16[128,512]{1,0:T(8,128)(2,1)S(1)}, bf16[128,512]{1,0:T(8,128)(2,1)}, u32[]{:S(2)}) copy-start(bf16[128,512]{1,0:T(8,128)(2,1)} %param.21) | copy-start | bytes 393220
  7.3 92.5 %copy-start.2 = (f32[128,128]{1,0:T(8,128)}, f32[128,128]{1,0:T(8,128)S(1)}, u32[]{:S(2)}) copy-start(f32[128,128]{1,0:T(8,128)S(1)} %get-tuple-element.158) | copy-start | bytes 196612
  7.3 0.7 copy-start.35
  8.3 0.7 copy-start.32
  8.3 0.7 copy-start.33
  9.0 166.3 %copy-start.28 = (s32[128]{0:T(128)}, s32[128]{0:T(128)S(1)}, u32[]{:S(2)}) copy-start(s32[128]{0:T(128)S(1)} %get-tuple-element.108) | copy-start | bytes 1540
  9.0 1.3 copy-start.34
  10.6 85.6 %copy-start.18 = (f32[8,128]{1,0:T(8,128)}, f32[8,128]{1,0:T(8,128)S(1)}, u32[]{:S(2)}) copy-start(f32[8,128]{1,0:T(8,128)S(1)} %convolution_bitcast_fusion.3) | copy-start | bytes 12292
  11.4 0.7 copy-start.25
  11.4 1.0 copy-start.10
  96.2 3.4 %copy-start.20 = (f32[8,128]{1,0:T(8,128)}, f32[8,128]{1,0:T(8,128)S(1)}, u32[]{:S(2)}) copy-start(f32[8,128]{1,0:T(8,128)S(1)} %get-tuple-element.135) | copy-start | bytes 12292
  99.5 120.0 %all-gather.6.cloned.1.call-start = ((), (), s32[]{:S(2)}) async-start(), calls=%async_computation | async-start | bytes 1310720 | tf_op jit(solution)/shard_map/all_gather | solution.py:25
  101.5 0.9 copy-start.11
  120.9 1.0 copy-start.22
  121.9 16.6 %copy-start.36 = (s32[8]{0:T(128)S(1)}, s32[8]{0:T(128)}, u32[]{:S(2)}) copy-start(s32[8]{0:T(128)} %param.37) | copy-start | bytes 100
  121.9 17.0 %copy-start.23 = (bf16[2,64,512]{2,1,0:T(8,128)(2,1)S(1)}, bf16[2,64,512]{2,1,0:T(8,128)(2,1)}, u32[]{:S(2)}) copy-start(bf16[2,64,512]{2,1,0:T(8,128)(2,1)} %param.33) | copy-start | bytes 393220
  138.9 16.8 %copy-start.24 = (bf16[128,512]{1,0:T(8,128)(2,1)S(1)}, bf16[128,512]{1,0:T(8,128)(2,1)}, u32[]{:S(2)}) copy-start(bf16[128,512]{1,0:T(8,128)(2,1)} %param.31) | copy-start | bytes 393220
  155.7 16.5 %copy-start.12 = (bf16[128,1024]{1,0:T(8,128)(2,1)S(1)}, bf16[128,1024]{1,0:T(8,128)(2,1)}, u32[]{:S(2)}) copy-start(bf16[128,1024]{1,0:T(8,128)(2,1)} %param.29) | copy-start | bytes 786436
  172.5 1.0 copy-start.16
  175.2 1.0 copy-start.5
  175.2 1.0 copy-start.14
  175.3 0.9 copy-start.8
  176.2 0.9 copy-start.7
  177.7 0.6 copy-start.26
  178.2 1.9 copy-start.6
  178.9 0.7 copy-start.37
  180.1 3.6 %copy-start.4 = (f32[128,4,256]{2,0,1:T(8,128)S(1)}, f32[128,4,256]{2,0,1:T(8,128)}, u32[]{:S(2)}) copy-start(f32[128,4,256]{2,0,1:T(8,128)} %copy.164) | copy-start | bytes 1572868
  183.7 2.3 copy-start.9
  186.0 0.6 copy-start.39
  186.0 9.2 %copy-start.3 = (f32[128,128]{1,0:T(8,128)S(1)}, f32[128,128]{1,0:T(8,128)}, u32[]{:S(2)}) copy-start(f32[128,128]{1,0:T(8,128)} %copy-done.2) | copy-start | bytes 196612
  197.5 0.9 copy-start.17
  198.4 0.9 copy-start.13
  199.7 15.2 %copy-start.29 = (s32[128]{0:T(128)S(1)}, s32[128]{0:T(128)}, u32[]{:S(2)}) copy-start(s32[128]{0:T(128)} %copy-done.28) | copy-start | bytes 1540
  215.4 0.7 copy-start.19
  217.3 1.5 copy-start.21
  219.6 0.6 copy-start.38
  231.4 0.6 copy-start.27
  232.0 0.7 copy-start.31
  232.7 1.0 copy-start.1
  234.5 0.7 copy-start.30
Sparse Core Ops, SparseCore 0:
  99.7 32.8 all-gather.7
  134.7 33.2 all-gather.5
where the time goes:
time: 244 us; the launch traced here: 243 us
  blocking collectives  90.3 us (37%)
  other arithmetic  87.6 us (36%)
  local copies, waits for them, and re-layouts  27.8 us (11%)
  matrix products  19.2 us (8%)
  between operations  16.1 us (7%)
    another operation x2, other arithmetic, shards(): jax.scipy.linalg.solve_triangular(system, jnp.concatenate([solve_values,...  79.4 us
    all_gather x1, blocking collectives, shards(): values = lax.all_gather(cached_value, 'context', axis=0, tiled=True)  16.8 us
    all_gather x1, blocking collectives, shards(): search_handles = lax.all_gather(new_key, 'context', axis=0, tiled=True)  16.7 us
    all_gather x1, blocking collectives, shards(): search_handles = lax.all_gather(cached_key, 'context', axis=0, tiled=True)  16.6 us
    all_gather x1, blocking collectives, shards(): values = lax.all_gather(new_value, 'context', axis=0, tiled=True)  16.5 us
    unnamed x91, local copies, waits for them, and re-layouts  15.3 us
    all_gather x1, blocking collectives, shards(): lax.all_gather(prefix_state, 'context', axis=2, tiled=True)  15.1 us
    unnamed x1, blocking collectives  8.58 us
  transfers between devices with their start and end apart: 2, of which 0 were waited for; matrix products, arithmetic and copies ran while one was open for 9% of the time, Pallas kernels for 0%

commit v1 on v0

--- a/solution.py
+++ b/solution.py
@@ -263,8 +263,13 @@
     flat_keys = search_handles.reshape(count * width, search_handles.shape[2])
     flat_values = values.reshape(count * width, values.shape[2])
     state = absorb(state, query_rot, flat_keys, flat_values, visible)
-    search_handles = lax.all_gather(new_key, "context", axis=0, tiled=True)
-    values = lax.all_gather(new_value, "context", axis=0, tiled=True)
+    search_handles, values = jnp.split(
+        lax.all_gather(
+            jnp.concatenate([new_key, new_value], axis=1), "context", axis=0, tiled=True
+        ),
+        [new_key.shape[1]],
+        axis=1,
+    )
     key_rows = jnp.arange(search_handles.shape[0], dtype=jnp.int32)
     key_segment = row_layout(key_rows, req_len, req_prefix, req_offset)[0]
     visible = (key_segment[None, :] == segment[:, None]) & (key_rows[None, :] <= rows[:, None])

time: 244 us -> 229 us (0.939)
  blocking collectives: 90.3 us -> 81.3 us
  matrix products: 19.2 us -> 15.6 us
    all_gather x2 -> x1, blocking collectives: 33.2 us -> 26.4 us  [shards(): lax.all_gather(jnp.concatenate([new_key, new_value], axis=1), 'context',...]
    dot_general x2, matrix products: 3.44 us -> 0.73 us  [absorb(): jnp.einsum('thn,nd->thd', weights.astype(jnp.bfloat16), values, preferred...]
    unnamed x91 -> x88, local copies, waits for them, and re-layouts: 15.3 us -> 14 us
  transfers between devices with their start and end apart: 2 -> 2, of which waited for: 0 -> 0; matrix products, arithmetic and copies ran while one was open for 9% -> 8% of each run, Pallas kernels for 0% -> 0%
where the time goes in v1:
time: 229 us; the launch traced here: 228 us
  other arithmetic  86.2 us (38%)
  blocking collectives  81.3 us (36%)
  local copies, waits for them, and re-layouts  26.6 us (12%)
  between operations  16.1 us (7%)
  matrix products  15.6 us (7%)
    another operation x2, other arithmetic, shards(): jax.scipy.linalg.solve_triangular(system, jnp.concatenate([solve_values,...  78.6 us
    all_gather x1, blocking collectives, shards(): lax.all_gather(jnp.concatenate([new_key, new_value], axis=1), 'context',...  26.4 us
    all_gather x1, blocking collectives, shards(): values = lax.all_gather(cached_value, 'context', axis=0, tiled=True)  16.1 us
    all_gather x1, blocking collectives, shards(): lax.all_gather(prefix_state, 'context', axis=2, tiled=True)  15.1 us
    all_gather x1, blocking collectives, shards(): search_handles = lax.all_gather(cached_key, 'context', axis=0, tiled=True)  15 us
    unnamed x88, local copies, waits for them, and re-layouts  14 us
    unnamed x1, blocking collectives  8.71 us
    dynamic_slice x12, local copies, waits for them, and re-layouts, one(): lax.dynamic_index_in_dim(a, turn, 0, False).astype(own.dtype)  6.04 us
  transfers between devices with their start and end apart: 2, of which 0 were waited for; matrix products, arithmetic and copies ran while one was open for 8% of the time, Pallas kernels for 0%

profile of v1, /device:TPU:26, one launch (start us, length us, event | category | flops | bytes accessed | tf_op | source)
XLA Modules:
  0.0 228.1 jit_solution(6046770942358816804)
XLA Ops:
  7.3 0.7 copy-done.34
  8.3 0.6 fusion.71
  8.9 0.7 select_reduce_fusion.1
  9.6 0.6 fusion.72
  11.8 0.6 copy-done.21
  13.3 1.3 fusion.15
  14.6 78.6 %custom-call.4 = f32[8,1,128,128]{2,3,1,0:T(8,128)S(1)} custom-call(f32[8,1,128,128]{3,2,1,0:T(8,128)S(1)} %fusion.15), custom_call_target="InvertDiagBlocksLowerTriangular" | custom-call | tf_op jit(solution)/shard_map/jit(_solve_triangular)/vmap()/triangular_solve | solution.py:177
  93.2 1.8 compare_and_fusion.3
  95.6 1.0 fusion.22
  96.6 1.7 convolution_convert_fusion
  98.6 1.7 fusion.20
  100.5 0.8 copy-done.7
  101.7 0.8 slice.68
  103.3 26.4 %all_gather.39 = bf16[512,512]{0,1:T(8,128)(2,1)} all-gather(bf16[128,512]{0,1:T(8,128)(2,1)S(1)} %pad_maximum_fusion.1), channel_id=1, replica_groups=mesh['group'=2,'context'=4,'head'=4] {'context'}, dimensions={0}, use_global_device_ids=true | all-gather | bytes 655360 | tf_op jit(solution)/shard_map/all_gather | solution.py:267
  130.0 15.0 %all_gather.37 = bf16[8,64,256]{2,1,0:T(8,128)(2,1)} all-gather(bf16[2,64,256]{2,1,0:T(8,128)(2,1)S(1)} %constant_dynamic-slice_fusion.3), channel_id=1, replica_groups=mesh['group'=2,'context'=4,'head'=4] {'context'}, dimensions={0}, use_global_device_ids=true | all-gather | bytes 327680 | tf_op jit(solution)/shard_map/all_gather | solution.py:250
  145.2 0.7 add.226
  146.0 0.7 eq.150
  146.7 16.1 %all_gather.38 = bf16[8,64,256]{2,1,0:T(8,128)(2,1)S(1)} all-gather(bf16[2,64,256]{2,1,0:T(8,128)(2,1)S(1)} %constant_dynamic-slice_fusion.2), channel_id=1, replica_groups=mesh['group'=2,'context'=4,'head'=4] {'context'}, dimensions={0}, use_global_device_ids=true | all-gather | bytes 327680 | tf_op jit(solution)/shard_map/all_gather | solution.py:251
  163.1 1.0 copy.166
  164.2 0.8 multiply_reduce_fusion.2
  168.8 0.6 copy-done.36
  169.5 0.6 dynamic-slice
  170.4 0.7 copy-done.3
  171.5 0.8 dynamic-update-slice
  172.3 8.7 %all-reduce = bf16[4]{0:T(256)(128)(2,1)} all-reduce(bf16[4]{0:T(256)(128)(2,1)S(1)} %dynamic-update-slice), channel_id=1, replica_groups=mesh['group'=2,'context'=4,'head'=4] {'context'}, use_global_device_ids=true, to_apply=%add | all-reduce | flops 4 | bytes 16
  181.2 0.9 copy.169
  182.3 0.9 copy-done.13
  183.2 0.9 copy-done.9
  184.5 15.1 %all_gather.36 = bf16[2,8,128,128]{3,2,0,1:T(8,128)(2,1)S(1)} all-gather(bf16[2,8,32,128]{3,2,0,1:T(8,128)(2,1)S(1)} %copy.150), channel_id=1, replica_groups=mesh['group'=2,'context'=4,'head'=4] {'context'}, dimensions={2}, use_global_device_ids=true | all-gather | bytes 655360 | tf_op jit(solution)/shard_map/all_gather | solution.py:216
  199.7 0.5 compare_convert_fusion
  200.2 0.6 copy-done.15
  200.9 1.2 convolution_multiply_fusion.3
  202.1 1.5 fusion.43
  203.5 0.7 convolution_subtract_fusion.1
  204.4 0.6 copy-done.37
  204.9 11.2 %while.14 = (s32[]{:T(128)}, f32[8,128,128]{1,2,0:T(8,128)S(1)}, f32[8,128,128]{1,2,0:T(8,128)S(1)}, s32[]{:T(128)}, bf16[4]{0:T(256)(128)(2,1)S(1)}, /*index=5*...) while((s32[]{:T(128)}, f32[8,128,128]{1,2,0:T(8,128)S(1)}, ...), condition=%wide.region_6.7_spmd, body=%wide.region_5.6_spmd.sunk | while | flops 403308544 | bytes 7340196 | solution.py:41
  204.9 1.1 constant_dynamic-slice_fusion.7
  206.2 0.6 dynamic_slice.39
  208.7 1.1 constant_dynamic-slice_fusion.7
  209.9 0.6 dynamic_slice.39
  212.4 1.1 constant_dynamic-slice_fusion.7
  213.7 0.6 dynamic_slice.39
  216.2 0.6 copy-done.26
  216.8 0.7 fusion.21
  217.9 0.7 copy-done.1
  218.6 0.8 multiply_reduce_fusion
  219.4 0.6 copy-done.29
  220.5 0.9 copy.168
  (164 shorter events, 14.8 us)
Async XLA Ops:
  7.2 122.8 %copy-start = (bf16[2,64,512]{2,1,0:T(8,128)(2,1)S(1)}, bf16[2,64,512]{2,1,0:T(8,128)(2,1)}, u32[]{:S(2)}) copy-start(bf16[2,64,512]{2,1,0:T(8,128)(2,1)} %param.32) | copy-start | bytes 393220
  7.2 197.1 %all-gather.7.cloned.1.call-start = ((), (), s32[]{:S(2)}) async-start(), calls=%async_computation.1 | async-start | bytes 1310720 | tf_op jit(solution)/shard_map/all_gather | solution.py:25
  7.2 4.0 %copy-start.11 = (bf16[128,512]{1,0:T(8,128)(2,1)S(1)}, bf16[128,512]{1,0:T(8,128)(2,1)}, u32[]{:S(2)}) copy-start(bf16[128,512]{1,0:T(8,128)(2,1)} %param.21) | copy-start | bytes 393220
  7.3 0.7 copy-start.34
  8.3 0.7 copy-start.31
  8.3 0.7 copy-start.32
  9.6 93.2 %copy-start.24 = (s32[128]{0:T(128)}, s32[128]{0:T(128)S(1)}, u32[]{:S(2)}) copy-start(s32[128]{0:T(128)S(1)} %get-tuple-element.106) | copy-start | bytes 1540
  9.6 1.2 copy-start.33
  11.0 84.0 %copy-start.14 = (f32[8,128]{1,0:T(8,128)}, f32[8,128]{1,0:T(8,128)S(1)}, u32[]{:S(2)}) copy-start(f32[8,128]{1,0:T(8,128)S(1)} %convolution_bitcast_fusion.3) | copy-start | bytes 12292
  11.8 0.7 copy-start.21
  11.8 1.0 copy-start.6
  95.1 3.4 %copy-start.16 = (f32[8,128]{1,0:T(8,128)}, f32[8,128]{1,0:T(8,128)S(1)}, u32[]{:S(2)}) copy-start(f32[8,128]{1,0:T(8,128)S(1)} %get-tuple-element.135) | copy-start | bytes 12292
  98.4 105.9 %all-gather.5.cloned.1.call-start = ((), (), s32[]{:S(2)}) async-start(), calls=%async_computation | async-start | bytes 1310720 | tf_op jit(solution)/shard_map/all_gather | solution.py:25
  100.3 0.9 copy-start.7
  101.7 0.9 copy-start.19
  101.7 1.0 copy-start.20
  130.0 15.0 %copy-start.35 = (s32[8]{0:T(128)S(1)}, s32[8]{0:T(128)}, u32[]{:S(2)}) copy-start(s32[8]{0:T(128)} %param.37) | copy-start | bytes 100
  130.0 16.6 %copy-start.18 = (bf16[2,64,512]{2,1,0:T(8,128)(2,1)S(1)}, bf16[2,64,512]{2,1,0:T(8,128)(2,1)}, u32[]{:S(2)}) copy-start(bf16[2,64,512]{2,1,0:T(8,128)(2,1)} %param.33) | copy-start | bytes 393220
  145.0 17.7 %copy-start.8 = (bf16[128,1024]{1,0:T(8,128)(2,1)S(1)}, bf16[128,1024]{1,0:T(8,128)(2,1)}, u32[]{:S(2)}) copy-start(bf16[128,1024]{1,0:T(8,128)(2,1)} %param.29) | copy-start | bytes 786436
  163.1 1.0 copy-start.12
  165.0 1.6 copy-start.2
  165.7 0.7 copy-start.22
  165.7 0.7 copy-start.23
  165.7 1.0 copy-start.10
  165.8 0.6 copy-start.25
  165.8 0.7 copy-start.27
  166.7 0.9 copy-start.4
  168.8 0.7 copy-start.36
  170.0 1.0 copy-start.3
  171.1 1.2 copy-start.5
  182.3 0.9 copy-start.13
  183.2 0.9 copy-start.9
  184.5 15.2 %copy-start.28 = (s32[128]{0:T(128)S(1)}, s32[128]{0:T(128)}, u32[]{:S(2)}) copy-start(s32[128]{0:T(128)} %get-tuple-element.108) | copy-start | bytes 1540
  200.2 0.7 copy-start.15
  202.1 1.5 copy-start.17
  204.3 0.6 copy-start.37
  216.2 0.7 copy-start.26
  216.8 0.7 copy-start.30
  217.5 1.0 copy-start.1
  219.4 0.7 copy-start.29
Sparse Core Ops, SparseCore 0:
  98.5 34.6 all-gather.6
  135.3 31.6 all-gather.4
